TPU v7x, 32 devices: a whole 2x2x4 slice. The times are simulated.
32 devices in a mesh: elem: 8 (over y, x, core), mode: 4 (over z).
Axes of the slice: x: 2, y: 2, z: 4, core: 2. Of those that a mesh axis runs over, the one named last changes fastest.
Arguments:
- velocity: float32 [3, 5184, 2, 512], P(None, 'elem', None, 'mode'), may hold values from -3 to 3
- column_width: float32 [8], P('elem'), may hold values from 0.5 to 2
- row_height: float32 [8], replicated, may hold values from 0.5 to 2
- disc_mask: int32 [64], P('elem'), may hold values from 0 to 1, as said below
Outputs:
- velocity_new: float32 [3, 5184, 2, 512], P(None, 'elem', None, 'mode')
Inputs may be any that keep to these rules, and one draw needn't show every extreme that they name: `disc_mask`: in each column of 8 elements the ones form one run of 2 to 4 consecutive rows, counted cyclically in y.
All inputs are finite; a program needn't handle non-finite values.
Results may differ from a plain program's by a relative error of at most 0.0001.
Values sent between devices are 32-bit elements; how exact they have to be, the bound alone decides.
A program may use at most 128 MiB of HBM per device.

v0:
```python
import math
import jax
import jax.numpy as jnp
import numpy as np
from jax import lax
from jax.sharding import PartitionSpec as P

ORDER = 8
ITERS = 2
gll_points = [
    -1.0,
    -0.8997579954114602,
    -0.6771862795107377,
    -0.3631174638261782,
    0.0,
    0.3631174638261782,
    0.6771862795107377,
    0.8997579954114602,
    1.0,
]
gll_weights = [
    0.0277777777777778,
    0.1654953615608055,
    0.2745387125001617,
    0.3464285109730463,
    0.3715192743764172,
    0.3464285109730463,
    0.2745387125001617,
    0.1654953615608055,
    0.0277777777777778,
]
viscosity = 0.5
time_step = 0.02
thrust_coef = 4.0 / 3.0
highest = lax.Precision.HIGHEST


def padded(shard, sides, width):
    for axis, dim in sides:
        peers, length = (lax.axis_size(axis), shard.shape[dim])
        up = [(i, (i + 1) % peers) for i in range(peers)]
        down = [(j, i) for i, j in up]
        last = lax.slice_in_dim(shard, length - width, length, axis=dim)
        initial = lax.slice_in_dim(shard, 0, width, axis=dim)
        before = lax.ppermute(last, axis, up)
        after = lax.ppermute(initial, axis, down)
        shard = jnp.concatenate([before, shard, after], axis=dim)
    return shard


def node_tables():
    points = np.array(gll_points)
    identity = np.eye(9)
    differences = points[:, None] - points[None, :] + identity
    barycentric = 1.0 / np.prod(differences, axis=1)
    off_diagonal = barycentric[None, :] / barycentric[:, None] / differences * (1.0 - identity)
    derivative = off_diagonal - identity * off_diagonal.sum(axis=1)[:, None]
    return (
        jnp.asarray(derivative, dtype=jnp.float32),
        jnp.asarray(np.array(gll_weights), dtype=jnp.float32),
    )


def spectral_tables(mode_count):
    planes = 3 * mode_count
    wave_index = jnp.arange(mode_count, dtype=jnp.int32)
    plane_index = jnp.arange(planes, dtype=jnp.int32)
    phase_index = wave_index[:, None] * plane_index[None, :] % planes
    angles = 2.0 * math.pi / planes * phase_index.astype(jnp.float32)
    cosine_table = jnp.cos(angles)
    sine_table = jnp.sin(angles)
    mode_weight = jnp.where(wave_index == 0, 1.0, 2.0).astype(jnp.float32)[:, None] / math.sqrt(
        mode_count
    )
    wave_number = 8.0 / mode_count * wave_index.astype(jnp.float32)[:, None]
    inverse = jnp.concatenate([mode_weight * cosine_table, -mode_weight * sine_table], axis=0)
    spanwise = jnp.concatenate(
        [-wave_number * mode_weight * sine_table, -wave_number * mode_weight * cosine_table], axis=0
    )
    forward = (
        math.sqrt(mode_count) / planes * jnp.concatenate([cosine_table, -sine_table], axis=0).T
    )
    return (inverse, spanwise, forward)


def assemble(nodal_field):
    extended = padded(nodal_field, (("elem", 2),), 1)
    first_layer = nodal_field[:, :, 0] + extended[:, :, 0]
    last_layer = nodal_field[:, :, 8] + extended[:, :, 10]
    nodal_field = jnp.concatenate(
        [first_layer[:, :, None], nodal_field[:, :, 1:8], last_layer[:, :, None]], axis=2
    )
    upper_layer = nodal_field[:, :, :, 8] + jnp.roll(nodal_field[:, :, :, 0], -1, axis=1)
    return jnp.concatenate(
        [
            jnp.roll(upper_layer, 1, axis=1)[:, :, :, None],
            nodal_field[:, :, :, 1:8],
            upper_layer[:, :, :, None],
        ],
        axis=3,
    )


def apply_operator(nodal_field, derivative, quad_weights, ratio_x, ratio_y, jacobian, factor):
    grad_r = jnp.einsum("ij,pejbl->peibl", derivative, nodal_field, precision=highest)
    grad_s = jnp.einsum("ij,peajl->peail", derivative, nodal_field, precision=highest)
    flux_r = grad_r * quad_weights[None, None, :, :, None] * ratio_x[None, :, None, None, None]
    flux_s = grad_s * quad_weights[None, None, :, :, None] * ratio_y[None, :, None, None, None]
    stiffness = jnp.einsum("ji,pejbl->peibl", derivative, flux_r, precision=highest) + jnp.einsum(
        "ji,peajl->peail", derivative, flux_s, precision=highest
    )
    masses = (
        jacobian[None, :, None, None, None] * quad_weights[None, None, :, :, None] * nodal_field
    )
    return assemble(factor * masses + viscosity * stiffness)


def weighted_sum(left_field, right_field, multiplicity):
    return jnp.sum(left_field * right_field * multiplicity[None, None, :, :, None], axis=(1, 2, 3))


def paired(residual, image_field, multiplicity):
    return lax.psum(
        (
            weighted_sum(residual, residual, multiplicity),
            weighted_sum(residual, image_field, multiplicity),
        ),
        "elem",
    )


def on_device(velocity, column_width, row_height, disc_mask):
    derivative, weights = node_tables()
    quad_weights = weights[:, None] * weights[None, :]
    node_index = jnp.arange(9)
    edge_count = jnp.where((node_index == 0) | (node_index == 8), 2.0, 1.0).astype(jnp.float32)
    multiplicity = 1.0 / (edge_count[:, None] * edge_count[None, :])
    groups = lax.axis_size("mode")
    local_modes = velocity.shape[3]
    mode_count = groups * local_modes
    planes = 3 * mode_count
    elements = velocity.shape[1] // 81
    local_elems = elements // groups
    col_width = column_width[0]
    inverse, spanwise, forward = spectral_tables(mode_count)
    nodal_field = velocity.reshape(3, elements, 9, 9, 2 * local_modes)
    mode_index = lax.axis_index("mode") * local_modes + jnp.arange(local_modes, dtype=jnp.int32)
    wavenumber = 8.0 / mode_count * mode_index.astype(jnp.float32)
    elem_start = lax.axis_index("mode") * local_elems
    local_heights = lax.dynamic_slice_in_dim(row_height, elem_start, local_elems)
    local_disc = lax.dynamic_slice_in_dim(disc_mask, elem_start, local_elems).astype(jnp.float32)
    members = lax.all_to_all(velocity, "mode", split_axis=1, concat_axis=3, tiled=True)
    flat_items = members.reshape(members.shape[0], members.shape[1], 2 * mode_count)
    values = jnp.einsum("pnl,lq->pnq", flat_items, inverse, precision=highest)
    along_z = jnp.einsum("pnl,lq->pnq", flat_items, spanwise, precision=highest)
    values = values.reshape(3, local_elems, 9, 9, planes)
    along_z = along_z.reshape(3, local_elems, 9, 9, planes)
    along_x = 2.0 / col_width * jnp.einsum("ij,pejbq->peibq", derivative, values, precision=highest)
    along_y = (2.0 / local_heights)[None, :, None, None, None] * jnp.einsum(
        "ij,peajq->peaiq", derivative, values, precision=highest
    )
    advection = values[0][None] * along_x + values[1][None] * along_y + values[2][None] * along_z
    plane_index = jnp.arange(planes)
    in_disc = ((plane_index >= 3 * planes // 8) & (plane_index < 5 * planes // 8)).astype(
        jnp.float32
    )
    disc_planes = 5 * planes // 8 - 3 * planes // 8
    local_jacobian = col_width * local_heights / 4.0
    node_weight = (local_disc * local_jacobian)[:, None, None] * quad_weights[None]
    partial_total = jnp.sum(node_weight[:, :, :, None] * values[0] * values[0] * in_disc)
    disc_total = lax.psum(partial_total, "mode")
    disc_area = disc_planes * col_width * jnp.sum(disc_mask.astype(jnp.float32) * row_height)
    pressure = disc_total / disc_area
    thrust = (
        -(0.5 * thrust_coef * ORDER)
        * pressure
        / col_width
        * local_disc[:, None, None, None]
        * in_disc
    )
    tendency = jnp.concatenate([(thrust - advection[0])[None], -advection[1:]], axis=0)
    spectral = jnp.einsum("peabq,ql->peabl", tendency, forward, precision=highest)
    spectral = spectral.reshape(3, local_elems * 81, 2, mode_count)
    returned = lax.all_to_all(spectral, "mode", split_axis=3, concat_axis=1, tiled=True)
    u_star = nodal_field + time_step * returned.reshape(3, elements, 9, 9, 2 * local_modes)
    jacobian = col_width * row_height / 4.0
    ratio_x = row_height / col_width
    ratio_y = col_width / row_height
    single = 1.0 / time_step + viscosity * wavenumber * wavenumber
    factor = jnp.concatenate([single, single])
    right_side = (
        assemble(
            jacobian[None, :, None, None, None] * quad_weights[None, None, :, :, None] * u_star
        )
        / time_step
    )
    residual = right_side
    solution = jnp.zeros_like(right_side)
    image_field = apply_operator(
        residual, derivative, quad_weights, ratio_x, ratio_y, jacobian, factor
    )
    norm_now, product = paired(residual, image_field, multiplicity)
    step_size = norm_now / product
    direction = residual
    along_image = image_field
    for iteration in range(ITERS):
        solution = solution + step_size[:, None, None, None, :] * direction
        residual = residual - step_size[:, None, None, None, :] * along_image
        if iteration + 1 < ITERS:
            image_field = apply_operator(
                residual, derivative, quad_weights, ratio_x, ratio_y, jacobian, factor
            )
            norm_next, product = paired(residual, image_field, multiplicity)
            beta_ratio = norm_next / norm_now
            step_size = norm_next / (product - beta_ratio * norm_next / step_size)
            direction = residual + beta_ratio[:, None, None, None, :] * direction
            along_image = image_field + beta_ratio[:, None, None, None, :] * along_image
            norm_now = norm_next
    return solution.reshape(3, elements * 81, 2, local_modes)


def solution(mesh):
    return jax.shard_map(
        on_device,
        mesh=mesh,
        in_specs=(P(None, "elem", None, "mode"), P("elem"), P(), P("elem")),
        out_specs=P(None, "elem", None, "mode"),
        check_vma=False,
    )
```

profile of v0, /device:TPU:0, one launch (start us, length us, event | category | flops | bytes accessed | tf_op | source)
XLA Modules:
  0.0 403.9 jit_solution(6718678095885858187)
XLA Ops:
  0.0 3.6 copy.119
  3.6 6.3 %all-to-all-start = ((f32[3,648,2,128]{3,2,0,1:T(2,128)}), f32[3,648,2,128]{3,2,0,1:T(2,128)S(1)}, u32[]{:S(2)}, u32[]{:S(2)}) async-start(f32[3,648,2,128]{3,2,0,1:T(2,128)} %copy.119), calls=%async_computation | async-start | bytes 3981312 | tf_op jit(solution)/shard_map/all_to_all | solution.py:152
  11.6 1.3 broadcast_divide_fusion.1
  13.6 14.0 %fusion.61 = (f32[512,1536]{1,0:T(8,128)}, f32[512,1536]{1,0:T(8,128)}) fusion(), kind=kLoop, calls=%fused_computation.87 | loop fusion | flops 7864320 | bytes 6291456 | tf_op jit(solution)/shard_map/cos | solution.py:70
  27.5 14.2 %fusion.63 = (f32[512,1536]{1,0:T(8,128)}, f32[512,1536]{1,0:T(8,128)}) fusion(f32[512]{0:T(512)S(1)} %negate_multiply_fusion), kind=kLoop, calls=%fused_computation.89 | loop fusion | flops 8650752 | bytes 6293504 | tf_op jit(solution)/shard_map/mul | solution.py:78
  41.7 14.2 %fusion.64 = (f32[512,1536]{1,0:T(8,128)}, f32[512,1536]{1,0:T(8,128)}) fusion(f32[512]{0:T(512)S(1)} %fusion.77, f32[512]{0:T(512)S(1)} %select_multiply_fusion), kind=kLoop, calls=%fused_computation.90 | loop fusion | flops 8650752 | bytes 6295552 | tf_op jit(solution)/shard_map/mul | solution.py:76
  55.9 1.8 copy.234
  57.7 3.6 reshape.205
  61.3 13.4 %fusion.54 = f32[3,162,1536]{2,1,0:T(8,128)S(1)} fusion(f32[3,162,1024]{2,1,0:T(8,128)} %reshape.205, f32[512,1536]{1,0:T(8,128)S(1)} %copy-done.11, f32[512,1536]{1,0:T(8,128)} %get-tuple-element.64), kind=kOutput, calls=%fused_computation.79 | convolution fusion | flops 9174515712 | bytes 11268096 | tf_op jit(solution)/shard_map/pnl,lq->pnq/dot_general | solution.py:154
  74.7 4.0 copy.122
  79.1 2.4 fusion.74
  82.3 2.5 mul.635
  84.8 2.1 copy.124
  86.9 2.5 mul.641
  89.5 3.5 copy.127
  92.9 13.4 %fusion.53 = f32[3,162,1536]{2,1,0:T(8,128)S(1)} fusion(f32[3,162,1024]{2,1,0:T(8,128)} %reshape.205, f32[512,1536]{1,0:T(8,128)} %get-tuple-element.56, f32[512,1536]{1,0:T(8,128)S(1)} %copy-done.10), kind=kOutput, calls=%fused_computation.78 | convolution fusion | flops 9174515712 | bytes 11268096 | tf_op jit(solution)/shard_map/pnl,lq->pnq/dot_general | solution.py:155
  106.4 4.2 %copy.128 = f32[3,162,1536]{2,0,1:T(4,128)} copy(f32[3,162,1536]{2,1,0:T(8,128)S(1)} %fusion.53) | data formatting | bytes 5971968 | tf_op jit(solution)/shard_map/pnl,lq->pnq/dot_general | solution.py:155
  110.6 12.8 %psum.35 = f32[]{:T(128)} all-reduce(f32[]{:T(128)} %get-tuple-element.35), channel_id=1, replica_groups=mesh['elem'=8,'mode'=4] {'mode'}, use_global_device_ids=true, to_apply=%region_1.2 | all-reduce | flops 1 | bytes 8 | tf_op jit(solution)/shard_map/psum | solution.py:171
  125.6 11.5 %fusion.16 = f32[3,2,9,1536,9]{3,4,2,1,0:T(8,128)} fusion(f32[9,9,1,1,1]{1,0,4,3,2:T(8,128)S(1)} %copy-done.13, f32[3,2,9,9,1536]{4,0,3,2,1:T(4,128)} %bitcast.137), kind=kOutput, calls=%fused_computation.24 | convolution fusion | flops 80621568 | bytes 5972292 | tf_op jit(solution)/shard_map/ij,peajq->peaiq/dot_general | solution.py:159
  137.1 14.2 %fusion.15 = f32[3,2,9,9,1536]{4,2,3,1,0:T(8,128)S(1)} fusion(f32[3,2,9,9,1536]{4,0,3,2,1:T(4,128)S(1)} %bitcast.139, f32[3,2,9,1536,9]{3,4,2,1,0:T(8,128)} %fusion.16, f32[9,9,1,1,1]{1,0,4,3,2:T(8,128)S(1)} %copy-done.13, f32[3,2,9,9,1536]{4,0,3,2,1:T(4,128)S(1)} %bitcast.138, f32[2,9,9,1536]{3,1,2,0:T(8,128)S(1)} %copy-done.3, f32[2]{0:T(128)S(1)} %copy-done.30, ...), kind=kOutput, calls=%fused_computation.20 | convolution fusion | flops 85847040 | bytes 14930256 | tf_op jit(solution)/shard_map/ij,pejbq->peibq/dot_general | solution.py:158
  152.0 1.2 copy-done.9
  153.3 1.1 copy-done.8
  154.3 17.1 %fusion.7 = f32[3,2,9,9,1024]{4,2,3,1,0:T(8,128)S(1)} fusion(f32[512,1536]{1,0:T(8,128)S(1)} %copy-done.9, f32[512,1536]{1,0:T(8,128)S(1)} %copy-done.8, f32[2,2,9,9,1536]{4,2,3,1,0:T(8,128)S(1)} %slice_negate_fusion, f32[1,2,9,9,1536]{4,2,3,1,0:T(8,128)S(1)} %slice_subtract_fusion), kind=kOutput, calls=%fused_computation.10 | convolution fusion | flops 9176835072 | bytes 11268096 | tf_op jit(solution)/shard_map/peabq,ql->peabl/dot_general | solution.py:182
  171.5 1.4 copy.131
  172.8 3.1 reshape.208
  176.0 6.6 %copy.132 = f32[3,162,2,512]{1,2,0,3:T(2,128)} copy(f32[3,162,2,512]{3,2,0,1:T(2,128)} %reshape.208) | data formatting | bytes 3981312 | tf_op jit(solution)/shard_map/reshape | solution.py:183
  182.5 4.7 %all-to-all-start.1 = ((f32[3,162,2,512]{1,2,0,3:T(2,128)}), f32[3,162,2,512]{1,2,0,3:T(2,128)}, u32[]{:S(2)}, u32[]{:S(2)}) async-start(f32[3,162,2,512]{1,2,0,3:T(2,128)} %copy.132), calls=%async_computation.1 | async-start | bytes 6291456 | tf_op jit(solution)/shard_map/all_to_all | solution.py:184
  187.2 3.2 reshape.217
  191.0 1.3 broadcast_multiply_fusion.2
  192.3 63.4 %all-to-all-done.1 = f32[3,162,2,512]{1,2,0,3:T(2,128)} async-done(((f32[3,162,2,512]{1,2,0,3:T(2,128)}), f32[3,162,2,512]{1,2,0,3:T(2,128)}, u32[]{:S(2)}, u32[]{:S(2)}) %all-to-all-start.1) | async-done | bytes 1990688 | tf_op jit(solution)/shard_map/all_to_all | solution.py:184
  255.6 5.2 %broadcast_multiply_fusion = f32[3,162,2,512]{1,2,0,3:T(2,128)} fusion(f32[3,162,2,512]{1,2,0,3:T(2,128)} %all-to-all-done.1), kind=kLoop, calls=%fused_computation.101 | loop fusion | flops 497664 | bytes 3981312 | tf_op jit(solution)/shard_map/mul | solution.py:185
  260.8 6.4 %copy.133 = f32[3,162,2,4,128]{4,2,0,1,3:T(2,128)} copy(f32[3,162,2,4,128]{1,2,0,4,3:T(2,128)} %bitcast.140) | data formatting | bytes 3981312 | tf_op jit(solution)/shard_map/mul | solution.py:185
  267.2 4.7 %mul.655 = f32[3,8,9,9,256]{4,0,3,2,1:T(4,128)} reshape(f32[3,4,162,2,128]{4,3,0,2,1:T(2,128)} %bitcast.143) | data formatting | bytes 3981312 | tf_op jit(solution)/shard_map/mul | solution.py:185
  271.9 3.3 fusion.36
  275.6 2.6 collective-permute-start.1
  278.5 3.9 collective-permute-done
  285.0 4.9 %fusion.44 = f32[3,8,9,256,9]{3,4,2,1,0:T(8,128)S(1)} fusion(f32[9,9,1,1,1]{1,0,4,3,2:T(8,128)S(1)} %copy-done.13, f32[3,8,9,9,256]{4,2,3,1,0:T(8,128)S(1)} %copy_multiply_fusion.4), kind=kOutput, calls=%fused_computation.64 | convolution fusion | flops 53747712 | bytes 3981636 | tf_op jit(solution)/shard_map/ij,peajl->peail/dot_general | solution.py:106
  290.0 4.2 %fusion.33 = f32[3,8,9,256,9]{3,4,2,1,0:T(8,128)S(1)} fusion(f32[9,9,1,1,1]{1,0,4,3,2:T(8,128)S(1)} %copy-done.13, f32[3,8,9,256,9]{3,4,2,1,0:T(8,128)S(1)} %fusion.44, f32[8]{0:T(128)S(1)} %copy-done.31, f32[9,9]{1,0:T(8,128)S(1)} %copy-done.17), kind=kOutput, calls=%fused_computation.49 | convolution fusion | flops 54743040 | bytes 3981992 | tf_op jit(solution)/shard_map/ji,peajl->peail/dot_general | solution.py:109
  294.2 3.9 fusion.35
  298.2 5.9 %fusion.32 = f32[3,8,9,9,256]{4,2,0,1,3:T(8,128)S(1)} fusion(f32[3,8,9,256,9]{3,4,2,1,0:T(8,128)S(1)} %fusion.33, f32[8,9,9]{1,0,2:T(8,128)S(1)} %copy-done.22, f32[256]{0:T(256)S(1)} %pad_maximum_fusion.6, f32[3,8,9,1,256]{4,2,0,1,3:T(8,128)S(1)} %maximum_add_fusion.1, f32[3,8,1,9,256]{4,2,0,1,3:T(1,128)S(1)} %get-tuple-element.32, ...), kind=kOutput, calls=%fused_computation.48 | convolution fusion | flops 61212672 | bytes 8408932 | tf_op jit(solution)/shard_map/ji,pejbl->peibl/dot_general | solution.py:109
  304.3 1.8 collective-permute-start.2
  306.1 1.1 collective-permute-start.3
  307.5 4.4 %collective-permute-done.2 = f32[3,8,1,9,256]{4,2,0,1,3:T(1,128)S(1)} collective-permute-done((f32[3,8,1,9,256]{4,2,0,1,3:T(1,128)S(1)}, f32[3,8,1,9,256]{4,2,0,1,3:T(1,128)S(1)}, u32[]{:S(2)}, u32[]{:S(2)}) %collective-permute-start.2) | collective-permute-done | bytes 221216 | tf_op jit(solution)/shard_map/ppermute | solution.py:45
  314.6 1.9 multiply_reduce_fusion.1
  316.5 14.7 %all-reduce.1 = (f32[3,256]{1,0:T(4,128)}, f32[3,256]{1,0:T(4,128)}) all-reduce(f32[3,256]{1,0:T(4,128)} %get-tuple-element.8, f32[3,256]{1,0:T(4,128)} %get-tuple-element.7), channel_id=1, replica_groups=mesh['elem'=8,'mode'=4] {'elem'}, use_global_device_ids=true, to_apply=%region_4.5 | all-reduce | flops 1536 | bytes 12288 | tf_op jit(solution)/shard_map/psum | solution.py:123
  331.2 1.3 broadcast_multiply_fusion.8
  332.5 5.0 %multiply_subtract_fusion = (f32[3,8,9,9,256]{4,2,3,1,0:T(8,128)S(1)}, f32[3,8,9,9,256]{4,2,3,1,0:T(8,128)}) fusion(f32[3,256]{1,0:T(4,128)S(1)} %get-tuple-element.14, f32[3,8,9,9,256]{4,2,0,1,3:T(8,128)S(1)} %fusion.25, f32[3,8,9,1,256]{4,2,3,1,0:T(8,128)} %copy-done.7, f32[3,7,9,256]{3,2,0,1:T(8,128)} %copy-done.12, f32[3,1,9,256]{3,2,0,1:T(8,128)} %copy-done.14, ...), kind=kLoop, calls=%fused_computation.72 | loop fusion | flops 2543616 | bytes 7965696 | tf_op jit(solution)/shard_map/sub | solution.py:208
  337.5 4.9 %fusion.39 = f32[3,8,9,256,9]{3,4,2,1,0:T(8,128)S(1)} fusion(f32[9,9,1,1,1]{1,0,4,3,2:T(8,128)S(1)} %copy-done.13, f32[3,8,9,9,256]{4,2,3,1,0:T(8,128)S(1)} %get-tuple-element.25), kind=kOutput, calls=%fused_computation.58 | convolution fusion | flops 53747712 | bytes 3981636 | tf_op jit(solution)/shard_map/ij,peajl->peail/dot_general | solution.py:106
  342.4 3.4 fusion.30
  345.9 4.1 %fusion.28 = f32[3,8,9,256,9]{3,4,2,1,0:T(8,128)S(1)} fusion(f32[9,9,1,1,1]{1,0,4,3,2:T(8,128)S(1)} %copy-done.13, f32[3,8,9,256,9]{3,4,2,1,0:T(8,128)S(1)} %fusion.39, f32[8]{0:T(128)S(1)} %copy-done.32, f32[9,9]{1,0:T(8,128)S(1)} %copy-done.18), kind=kOutput, calls=%fused_computation.42 | convolution fusion | flops 54743040 | bytes 3981992 | tf_op jit(solution)/shard_map/ji,peajl->peail/dot_general | solution.py:109
  350.0 5.2 %fusion.27 = f32[3,8,9,9,256]{4,2,0,1,3:T(8,128)S(1)} fusion(f32[3,8,9,256,9]{3,4,2,1,0:T(8,128)S(1)} %fusion.28, f32[3,8,9,9,256]{4,2,3,1,0:T(8,128)S(1)} %get-tuple-element.25, f32[9,9,1,1,1]{1,0,2,3,4:T(8,128)S(1)} %copy-done.29, f32[3,8,9,9,256]{4,2,3,1,0:T(8,128)S(1)} %fusion.30, f32[256]{0:T(256)S(1)} %copy-done.40, f32[8,9,9]{1,0,2:T(8,128)S(1)} %copy-done.15), kind=kOutput, calls=%fused_computation.41 | convolution fusion | flops 56236032 | bytes 7966564 | tf_op jit(solution)/shard_map/ji,pejbl->peibl/dot_general | solution.py:109
  355.3 1.9 copy-done.6
  358.2 2.6 collective-permute-start.5
  360.8 3.0 copy.136
  363.8 4.8 %concatenate.89 = f32[3,648,2,128]{3,2,0,1:T(2,128)} reshape(f32[3,8,9,9,256]{4,0,3,2,1:T(4,128)} %copy.136) | data formatting | bytes 3981312 | tf_op jit(solution)/shard_map/concatenate | solution.py:94
  368.6 1.7 slice.176
  370.3 5.0 %copy.155 = f32[3,8,9,9,256]{4,0,3,2,1:T(4,128)} copy(f32[3,8,9,9,256]{4,2,3,1,0:T(8,128)} %get-tuple-element.26) | data formatting | bytes 3981312 | tf_op jit(solution)/shard_map/concatenate | solution.py:94
  375.2 4.5 %concatenate.105 = f32[3,648,2,128]{3,2,0,1:T(2,128)} reshape(f32[3,8,9,9,256]{4,0,3,2,1:T(4,128)} %copy.155) | data formatting | bytes 3981312 | tf_op jit(solution)/shard_map/concatenate | solution.py:94
  379.8 2.5 slice_add_fusion.1
  382.7 1.6 copy-done.1
  384.3 1.3 fusion.38
  385.7 12.0 %all-reduce = (f32[3,256]{1,0:T(4,128)S(1)}, f32[3,256]{1,0:T(4,128)S(1)}) all-reduce(f32[3,256]{1,0:T(4,128)S(1)} %get-tuple-element.6, f32[3,256]{1,0:T(4,128)S(1)} %get-tuple-element.5), channel_id=1, replica_groups=mesh['elem'=8,'mode'=4] {'elem'}, use_global_device_ids=true, to_apply=%region_8.9 | all-reduce | flops 1536 | bytes 12288 | tf_op jit(solution)/shard_map/psum | solution.py:123
  397.8 3.6 multiply_add_fusion
  401.4 2.0 copy.156
  (142 shorter events, 12.8 us)
Async XLA Ops:
  0.0 10.6 %copy-start.37 = (f32[9]{0:T(128)S(1)}, f32[9]{0:T(128)}, u32[]{:S(2)}) copy-start(f32[9]{0:T(128)} %constant.72.clone) | copy-start | bytes 112
  0.0 10.7 %copy-start.38 = (f32[8]{0:T(128)S(1)}, f32[8]{0:T(128)}, u32[]{:S(2)}) copy-start(f32[8]{0:T(128)} %param.8) | copy-start | bytes 100
  0.0 10.7 %copy-start.35 = (s32[8]{0:T(128)S(1)}, s32[8]{0:T(128)}, u32[]{:S(2)}) copy-start(s32[8]{0:T(128)} %param.9) | copy-start | bytes 100
  3.6 52.3 %all-to-all-start = ((f32[3,648,2,128]{3,2,0,1:T(2,128)}), f32[3,648,2,128]{3,2,0,1:T(2,128)S(1)}, u32[]{:S(2)}, u32[]{:S(2)}) async-start(f32[3,648,2,128]{3,2,0,1:T(2,128)} %copy.119), calls=%async_computation | async-start | bytes 3981312 | tf_op jit(solution)/shard_map/all_to_all | solution.py:152
  10.7 31.0 %copy-start.16 = (f32[9,9]{1,0:T(8,128)}, f32[9,9]{1,0:T(8,128)S(1)}, u32[]{:S(2)}) copy-start(f32[9,9]{1,0:T(8,128)S(1)} %copy.118) | copy-start | bytes 976
  13.6 65.5 %copy-start.21 = (f32[1536]{0:T(1024)}, f32[1536]{0:T(1024)S(1)}, u32[]{:S(2)}) copy-start(f32[1536]{0:T(1024)S(1)} %fusion.76) | copy-start | bytes 18436
  57.7 3.6 copy-start.11
  89.5 3.5 copy-start.10
  106.3 19.2 %copy-start.13 = (f32[9,9,1,1,1]{1,0,4,3,2:T(8,128)S(1)}, f32[9,9,1,1,1]{1,0,4,3,2:T(8,128)}, u32[]{:S(2)}) copy-start(f32[9,9,1,1,1]{1,0,4,3,2:T(8,128)} %constant.74) | copy-start | bytes 976
  125.6 11.5 %copy-start.2 = (f32[3,162,1536]{2,0,1:T(4,128)S(1)}, f32[3,162,1536]{2,0,1:T(4,128)}, u32[]{:S(2)}) copy-start(f32[3,162,1536]{2,0,1:T(4,128)} %copy.122) | copy-start | bytes 8957956
  125.6 11.5 %copy-start.3 = (f32[2,9,9,1536]{3,1,2,0:T(8,128)S(1)}, f32[2,9,9,1536]{3,1,2,0:T(8,128)}, u32[]{:S(2)}) copy-start(f32[2,9,9,1536]{3,1,2,0:T(8,128)} %copy.127) | copy-start | bytes 2985988
  125.6 11.5 %copy-start.5 = (f32[3,162,1536]{2,0,1:T(4,128)S(1)}, f32[3,162,1536]{2,0,1:T(4,128)}, u32[]{:S(2)}) copy-start(f32[3,162,1536]{2,0,1:T(4,128)} %copy.128) | copy-start | bytes 8957956
  125.6 11.5 %copy-start.30 = (f32[2]{0:T(128)S(1)}, f32[2]{0:T(128)}, u32[]{:S(2)}) copy-start(f32[2]{0:T(128)} %get-tuple-element.62) | copy-start | bytes 28
  151.4 1.9 copy-start.9
  151.8 2.5 copy-start.8
  182.5 73.1 %all-to-all-start.1 = ((f32[3,162,2,512]{1,2,0,3:T(2,128)}), f32[3,162,2,512]{1,2,0,3:T(2,128)}, u32[]{:S(2)}, u32[]{:S(2)}) async-start(f32[3,162,2,512]{1,2,0,3:T(2,128)} %copy.132), calls=%async_computation.1 | async-start | bytes 6291456 | tf_op jit(solution)/shard_map/all_to_all | solution.py:184
  275.5 6.8 %collective-permute-start = (f32[3,8,1,9,256]{4,2,0,1,3:T(1,128)S(1)}, f32[3,8,1,9,256]{4,2,0,1,3:T(1,128)S(1)}, u32[]{:S(2)}, u32[]{:S(2)}) collective-permute-start(f32[3,8,1,9,256]{4,2,0,1,3:T(1,128)S(1)} %get-tuple-element.33), channel_id=1, source_target_pairs={{0,4},{4,8},{8,12},{12,16},{16,20},{20,24},{24,28},{28,0},{1,5},{5... | collective-permute-start | bytes 663560 | tf_op jit(solution)/shard_map/ppermute | solution.py:45
  275.6 6.8 %collective-permute-start.1 = (f32[3,8,1,9,256]{4,2,0,1,3:T(1,128)S(1)}, f32[3,8,1,9,256]{4,2,0,1,3:T(1,128)S(1)}, u32[]{:S(2)}, u32[]{:S(2)}) collective-permute-start(f32[3,8,1,9,256]{4,2,0,1,3:T(1,128)S(1)} %get-tuple-element.34), channel_id=1, source_target_pairs={{4,0},{8,4},{12,8},{16,12},{20,16},{24,20},{28,24},{0,28},{5,1},{9... | collective-permute-start | bytes 663560 | tf_op jit(solution)/shard_map/ppermute | solution.py:46
  278.2 19.9 %copy-start.39 = (f32[256]{0:T(256)}, f32[256]{0:T(256)S(1)}, u32[]{:S(2)}) copy-start(f32[256]{0:T(256)S(1)} %pad_maximum_fusion.6) | copy-start | bytes 3076
  285.0 4.9 %copy-start.17 = (f32[9,9]{1,0:T(8,128)S(1)}, f32[9,9]{1,0:T(8,128)}, u32[]{:S(2)}) copy-start(f32[9,9]{1,0:T(8,128)} %copy-done.16) | copy-start | bytes 976
  285.0 4.9 %copy-start.31 = (f32[8]{0:T(128)S(1)}, f32[8]{0:T(128)}, u32[]{:S(2)}) copy-start(f32[8]{0:T(128)} %get-tuple-element.57) | copy-start | bytes 100
  290.0 4.2 %copy-start.33 = (f32[8]{0:T(128)S(1)}, f32[8]{0:T(128)}, u32[]{:S(2)}) copy-start(f32[8]{0:T(128)} %get-tuple-element.60) | copy-start | bytes 100
  294.1 4.0 copy-start.22
  294.2 4.0 copy-start.28
  298.1 9.1 %copy-start.36 = (f32[9]{0:T(128)S(1)}, f32[9]{0:T(128)}, u32[]{:S(2)}) copy-start(f32[9]{0:T(128)} %or_select_fusion) | copy-start | bytes 112
  304.3 7.6 %collective-permute-start.2 = (f32[3,8,1,9,256]{4,2,0,1,3:T(1,128)S(1)}, f32[3,8,1,9,256]{4,2,0,1,3:T(1,128)S(1)}, u32[]{:S(2)}, u32[]{:S(2)}) collective-permute-start(f32[3,8,1,9,256]{4,2,0,1,3:T(1,128)S(1)} %get-tuple-element.29), channel_id=1, source_target_pairs={{0,4},{4,8},{8,12},{12,16},{16,20},{20,24},{24,28},{28,0},{1,5},{5... | collective-permute-start | bytes 663560 | tf_op jit(solution)/shard_map/ppermute | solution.py:45
  306.1 5.8 %collective-permute-start.3 = (f32[3,8,1,9,256]{4,2,0,1,3:T(1,128)S(1)}, f32[3,8,1,9,256]{4,2,0,1,3:T(1,128)S(1)}, u32[]{:S(2)}, u32[]{:S(2)}) collective-permute-start(f32[3,8,1,9,256]{4,2,0,1,3:T(1,128)S(1)} %get-tuple-element.30), channel_id=1, source_target_pairs={{4,0},{8,4},{12,8},{16,12},{20,16},{24,20},{28,24},{0,28},{5,1},{9... | collective-permute-start | bytes 663560 | tf_op jit(solution)/shard_map/ppermute | solution.py:46
  307.3 6.2 %copy-start.19 = (f32[9,9]{0,1:T(8,128)}, f32[9,9]{0,1:T(8,128)S(1)}, u32[]{:S(2)}) copy-start(f32[9,9]{0,1:T(8,128)S(1)} %multiply_divide_fusion) | copy-start | bytes 976
  313.1 1.5 copy-start.4
  313.4 3.1 copy-start.12
  313.4 3.0 copy-start.14
  314.6 1.9 copy-start.7
  332.5 5.0 %copy-start.23 = (f32[3,256]{1,0:T(4,128)}, f32[3,256]{1,0:T(4,128)S(1)}, u32[]{:S(2)}) copy-start(f32[3,256]{1,0:T(4,128)S(1)} %get-tuple-element.14) | copy-start | bytes 9220
  337.5 12.5 %copy-start = (f32[3,8,9,9,256]{4,2,3,1,0:T(8,128)}, f32[3,8,9,9,256]{4,2,3,1,0:T(8,128)S(1)}, u32[]{:S(2)}) copy-start(f32[3,8,9,9,256]{4,2,3,1,0:T(8,128)S(1)} %get-tuple-element.25) | copy-start | bytes 5971972
  337.5 4.9 %copy-start.34 = (f32[8]{0:T(128)S(1)}, f32[8]{0:T(128)}, u32[]{:S(2)}) copy-start(f32[8]{0:T(128)} %get-tuple-element.60) | copy-start | bytes 100
  342.4 3.4 copy-start.18
  342.4 3.4 copy-start.32
  345.8 4.2 %copy-start.15 = (f32[8,9,9]{1,0,2:T(8,128)S(1)}, f32[8,9,9]{1,0,2:T(8,128)}, u32[]{:S(2)}) copy-start(f32[8,9,9]{1,0,2:T(8,128)} %get-tuple-element.52) | copy-start | bytes 7780
  345.8 4.2 %copy-start.29 = (f32[9,9,1,1,1]{1,0,2,3,4:T(8,128)S(1)}, f32[9,9,1,1,1]{1,0,2,3,4:T(8,128)}, u32[]{:S(2)}) copy-start(f32[9,9,1,1,1]{1,0,2,3,4:T(8,128)} %constant.75) | copy-start | bytes 976
  345.9 4.2 %copy-start.40 = (f32[256]{0:T(256)S(1)}, f32[256]{0:T(256)}, u32[]{:S(2)}) copy-start(f32[256]{0:T(256)} %copy-done.39) | copy-start | bytes 3076
  355.3 1.9 copy-start.6
  358.2 21.6 %collective-permute-start.4 = (f32[3,8,1,9,256]{4,2,0,1,3:T(1,128)}, f32[3,8,1,9,256]{4,2,0,1,3:T(1,128)}, u32[]{:S(2)}, u32[]{:S(2)}) collective-permute-start(f32[3,8,1,9,256]{4,2,0,1,3:T(1,128)} %get-tuple-element.23), channel_id=1, source_target_pairs={{0,4},{4,8},{8,12},{12,16},{16,20},{20,24},{24,28},{28,0},{1,5},{5... | collective-permute-start | bytes 663560 | tf_op jit(solution)/shard_map/ppermute | solution.py:45
  358.2 21.6 %collective-permute-start.5 = (f32[3,8,1,9,256]{4,2,0,1,3:T(1,128)}, f32[3,8,1,9,256]{4,2,0,1,3:T(1,128)}, u32[]{:S(2)}, u32[]{:S(2)}) collective-permute-start(f32[3,8,1,9,256]{4,2,0,1,3:T(1,128)} %get-tuple-element.24), channel_id=1, source_target_pairs={{4,0},{8,4},{12,8},{16,12},{20,16},{24,20},{28,24},{0,28},{5,1},{9... | collective-permute-start | bytes 663560 | tf_op jit(solution)/shard_map/ppermute | solution.py:46
  363.8 6.5 %copy-start.24 = (f32[3,256]{1,0:T(4,128)S(1)}, f32[3,256]{1,0:T(4,128)}, u32[]{:S(2)}) copy-start(f32[3,256]{1,0:T(4,128)} %copy-done.23) | copy-start | bytes 9220
  375.2 4.5 %copy-start.25 = (f32[3,256]{1,0:T(4,128)S(1)}, f32[3,256]{1,0:T(4,128)}, u32[]{:S(2)}) copy-start(f32[3,256]{1,0:T(4,128)} %get-tuple-element.13) | copy-start | bytes 9220
  382.3 2.0 copy-start.1
  382.3 2.0 copy-start.20
  384.3 13.4 %copy-start.26 = (f32[3,256]{1,0:T(4,128)S(1)}, f32[3,256]{1,0:T(4,128)}, u32[]{:S(2)}) copy-start(f32[3,256]{1,0:T(4,128)} %get-tuple-element.11) | copy-start | bytes 9220
  384.3 13.4 %copy-start.27 = (f32[3,256]{1,0:T(4,128)S(1)}, f32[3,256]{1,0:T(4,128)}, u32[]{:S(2)}) copy-start(f32[3,256]{1,0:T(4,128)} %get-tuple-element.12) | copy-start | bytes 9220
where the time goes:
time: 409 us; the launch traced here: 404 us
  matrix products  106 us (26%)
  local copies, waits for them, and re-layouts  84.7 us (21%)
  other arithmetic  79.2 us (19%)
  waiting for transfers between devices  71.7 us (18%)
  blocking collectives  39.5 us (10%)
  starting transfers between devices  19.2 us (5%)
    all_to_all x1, waiting for transfers between devices, on_device(): lax.all_to_all(spectral, 'mode', split_axis=3, concat_axis=1, tiled=True)  63.4 us
    psum x2, blocking collectives, paired(): lax.psum((weighted_sum(residual, residual, multiplicity), weighted_sum(re...  26.7 us
    concatenate x4, local copies, waits for them, and re-layouts, assemble(): jnp.concatenate([jnp.roll(upper_layer, 1, axis=1)[:, :, :, None], nodal_f...  17.2 us
    dot_general x1, matrix products, on_device(): jnp.einsum('peabq,ql->peabl', tendency, forward, precision=highest)  17.1 us
    dot_general x1, matrix products, on_device(): jnp.einsum('ij,pejbq->peibq', derivative, values, precision=highest)  14.2 us
    mul x2, other arithmetic, spectral_tables(): -wave_number * mode_weight * sine_table  14.2 us
    mul x1, other arithmetic, spectral_tables(): -mode_weight * sine_table  14.2 us
    cos x1, other arithmetic, spectral_tables(): cosine_table = jnp.cos(angles)  14 us
  transfers between devices with their start and end apart: 8, of which 3 were waited for; matrix products, arithmetic and copies ran while one was open for 17% of the time, Pallas kernels for 0%

commit v1 on v0

--- a/solution.py
+++ b/solution.py
@@ -181,7 +181,10 @@
     tendency = jnp.concatenate([(thrust - advection[0])[None], -advection[1:]], axis=0)
     spectral = jnp.einsum("peabq,ql->peabl", tendency, forward, precision=highest)
     spectral = spectral.reshape(3, local_elems * 81, 2, mode_count)
-    returned = lax.all_to_all(spectral, "mode", split_axis=3, concat_axis=1, tiled=True)
+    returned = jnp.concatenate(
+        lax.all_to_all(jnp.stack(jnp.split(spectral, lax.axis_size("mode"), axis=3)), "mode", 0, 0),
+        axis=1,
+    )
     u_star = nodal_field + time_step * returned.reshape(3, elements, 9, 9, 2 * local_modes)
     jacobian = col_width * row_height / 4.0
     ratio_x = row_height / col_width

time: 409 us -> 374 us (0.914)
  waiting for transfers between devices: 71.7 us -> 47 us
  local copies, waits for them, and re-layouts: 84.7 us -> 73.9 us
    all_to_all x1, waiting for transfers between devices: 63.4 us -> 38.6 us  [on_device(): lax.all_to_all(jnp.stack(jnp.split(spectral, lax.axis_size('mode'), axis=...]
    reshape x2 -> x1, local copies, waits for them, and re-layouts: 9.69 us -> 3.12 us  [on_device(): spectral = spectral.reshape(3, local_elems * 81, 2, mode_count)]
    mul x2 -> x1, local copies, waits for them, and re-layouts: 11.1 us -> 4.67 us  [on_device(): time_step * returned.reshape(3, elements, 9, 9, 2 * local_modes)]
  transfers between devices with their start and end apart: 8 -> 8, of which waited for: 3 -> 4; matrix products, arithmetic and copies ran while one was open for 17% -> 19% of each run, Pallas kernels for 0% -> 0%
where the time goes in v1:
time: 374 us; the launch traced here: 369 us
  matrix products  106 us (28%)
  other arithmetic  79.8 us (21%)
  local copies, waits for them, and re-layouts  73.9 us (20%)
  waiting for transfers between devices  47 us (13%)
  blocking collectives  39.5 us (11%)
  starting transfers between devices  19 us (5%)
    all_to_all x1, waiting for transfers between devices, on_device(): lax.all_to_all(jnp.stack(jnp.split(spectral, lax.axis_size('mode'), axis=...  38.6 us
    psum x2, blocking collectives, paired(): lax.psum((weighted_sum(residual, residual, multiplicity), weighted_sum(re...  26.7 us
    concatenate x4, local copies, waits for them, and re-layouts, assemble(): jnp.concatenate([jnp.roll(upper_layer, 1, axis=1)[:, :, :, None], nodal_f...  17.2 us
    dot_general x1, matrix products, on_device(): jnp.einsum('peabq,ql->peabl', tendency, forward, precision=highest)  17.1 us
    dot_general x1, matrix products, on_device(): jnp.einsum('ij,pejbq->peibq', derivative, values, precision=highest)  14.2 us
    mul x1, other arithmetic, spectral_tables(): -mode_weight * sine_table  14.2 us
    mul x2, other arithmetic, spectral_tables(): -wave_number * mode_weight * sine_table  14.2 us
    cos x1, other arithmetic, spectral_tables(): cosine_table = jnp.cos(angles)  14 us
  transfers between devices with their start and end apart: 8, of which 4 were waited for; matrix products, arithmetic and copies ran while one was open for 19% of the time, Pallas kernels for 0%

profile of v1, /device:TPU:0, one launch (start us, length us, event | category | flops | bytes accessed | tf_op | source)
XLA Modules:
  0.0 368.7 jit_solution(5086426370864941260)
XLA Ops:
  0.0 3.6 copy.78
  3.6 6.3 %all-to-all-start = ((f32[3,648,2,128]{3,2,0,1:T(2,128)}), f32[3,648,2,128]{3,2,0,1:T(2,128)S(1)}, u32[]{:S(2)}, u32[]{:S(2)}) async-start(f32[3,648,2,128]{3,2,0,1:T(2,128)} %copy.78), calls=%async_computation | async-start | bytes 3981312 | tf_op jit(solution)/shard_map/all_to_all | solution.py:152
  11.5 1.2 broadcast_divide_fusion.1
  13.4 14.0 %fusion.61 = (f32[512,1536]{1,0:T(8,128)}, f32[512,1536]{1,0:T(8,128)}) fusion(), kind=kLoop, calls=%fused_computation.87 | loop fusion | flops 7864320 | bytes 6291456 | tf_op jit(solution)/shard_map/cos | solution.py:70
  27.4 14.2 %fusion.63 = (f32[512,1536]{1,0:T(8,128)}, f32[512,1536]{1,0:T(8,128)}) fusion(f32[512]{0:T(512)S(1)} %negate_multiply_fusion), kind=kLoop, calls=%fused_computation.89 | loop fusion | flops 8650752 | bytes 6293504 | tf_op jit(solution)/shard_map/mul | solution.py:78
  41.6 14.2 %fusion.64 = (f32[512,1536]{1,0:T(8,128)}, f32[512,1536]{1,0:T(8,128)}) fusion(f32[512]{0:T(512)S(1)} %fusion.77, f32[512]{0:T(512)S(1)} %select_multiply_fusion), kind=kLoop, calls=%fused_computation.90 | loop fusion | flops 8650752 | bytes 6295552 | tf_op jit(solution)/shard_map/mul | solution.py:76
  55.8 1.8 copy.195
  57.6 3.6 reshape.202
  61.2 13.4 %fusion.54 = f32[3,162,1536]{2,1,0:T(8,128)S(1)} fusion(f32[3,162,1024]{2,1,0:T(8,128)} %reshape.202, f32[512,1536]{1,0:T(8,128)S(1)} %copy-done.11, f32[512,1536]{1,0:T(8,128)} %get-tuple-element.68), kind=kOutput, calls=%fused_computation.79 | convolution fusion | flops 9174515712 | bytes 11268096 | tf_op jit(solution)/shard_map/pnl,lq->pnq/dot_general | solution.py:154
  74.6 4.0 %copy.81 = f32[3,162,1536]{2,0,1:T(4,128)} copy(f32[3,162,1536]{2,1,0:T(8,128)S(1)} %fusion.54) | data formatting | bytes 5971968 | tf_op jit(solution)/shard_map/pnl,lq->pnq/dot_general | solution.py:154
  79.0 2.4 fusion.74
  82.3 2.5 mul.632
  84.8 2.1 copy.83
  86.9 2.5 mul.638
  89.4 3.5 copy.86
  92.9 13.4 %fusion.53 = f32[3,162,1536]{2,1,0:T(8,128)S(1)} fusion(f32[3,162,1024]{2,1,0:T(8,128)} %reshape.202, f32[512,1536]{1,0:T(8,128)} %get-tuple-element.60, f32[512,1536]{1,0:T(8,128)S(1)} %copy-done.10), kind=kOutput, calls=%fused_computation.78 | convolution fusion | flops 9174515712 | bytes 11268096 | tf_op jit(solution)/shard_map/pnl,lq->pnq/dot_general | solution.py:155
  106.3 4.2 %copy.87 = f32[3,162,1536]{2,0,1:T(4,128)} copy(f32[3,162,1536]{2,1,0:T(8,128)S(1)} %fusion.53) | data formatting | bytes 5971968 | tf_op jit(solution)/shard_map/pnl,lq->pnq/dot_general | solution.py:155
  110.6 12.7 %psum.35 = f32[]{:T(128)} all-reduce(f32[]{:T(128)} %get-tuple-element.35), channel_id=1, replica_groups=mesh['elem'=8,'mode'=4] {'mode'}, use_global_device_ids=true, to_apply=%region_1.2 | all-reduce | flops 1 | bytes 8 | tf_op jit(solution)/shard_map/psum | solution.py:171
  125.5 11.5 %fusion.16 = f32[3,2,9,1536,9]{3,4,2,1,0:T(8,128)} fusion(f32[9,9,1,1,1]{1,0,4,3,2:T(8,128)S(1)} %copy-done.13, f32[3,2,9,9,1536]{4,0,3,2,1:T(4,128)} %bitcast.145), kind=kOutput, calls=%fused_computation.24 | convolution fusion | flops 80621568 | bytes 5972292 | tf_op jit(solution)/shard_map/ij,peajq->peaiq/dot_general | solution.py:159
  137.0 14.2 %fusion.15 = f32[3,2,9,9,1536]{4,2,3,1,0:T(8,128)S(1)} fusion(f32[3,2,9,9,1536]{4,0,3,2,1:T(4,128)S(1)} %bitcast.147, f32[3,2,9,1536,9]{3,4,2,1,0:T(8,128)} %fusion.16, f32[9,9,1,1,1]{1,0,4,3,2:T(8,128)S(1)} %copy-done.13, f32[3,2,9,9,1536]{4,0,3,2,1:T(4,128)S(1)} %bitcast.146, f32[2,9,9,1536]{3,1,2,0:T(8,128)S(1)} %copy-done.3, f32[2]{0:T(128)S(1)} %copy-done.30, ...), kind=kOutput, calls=%fused_computation.20 | convolution fusion | flops 85847040 | bytes 14930256 | tf_op jit(solution)/shard_map/ij,pejbq->peibq/dot_general | solution.py:158
  152.0 1.2 copy-done.9
  153.2 1.1 copy-done.8
  154.2 17.1 %fusion.7 = f32[3,2,9,9,1024]{4,2,3,1,0:T(8,128)S(1)} fusion(f32[512,1536]{1,0:T(8,128)S(1)} %copy-done.9, f32[512,1536]{1,0:T(8,128)S(1)} %copy-done.8, f32[2,2,9,9,1536]{4,2,3,1,0:T(8,128)S(1)} %slice_negate_fusion, f32[1,2,9,9,1536]{4,2,3,1,0:T(8,128)S(1)} %slice_subtract_fusion), kind=kOutput, calls=%fused_computation.10 | convolution fusion | flops 9176835072 | bytes 11268096 | tf_op jit(solution)/shard_map/peabq,ql->peabl/dot_general | solution.py:182
  171.4 1.4 copy.90
  172.8 3.1 reshape.205
  175.9 2.2 slice_bitcast_fusion.3
  178.0 2.0 pad_maximum_fusion.3
  180.1 4.4 %all-to-all-start.1 = ((f32[4,3,162,2,128]{4,3,1,2,0:T(2,128)}), f32[4,3,162,2,128]{4,3,1,2,0:T(2,128)}, u32[]{:S(2)}, u32[]{:S(2)}) async-start(f32[4,3,162,2,128]{4,3,1,2,0:T(2,128)} %pad_maximum_fusion.3), calls=%async_computation.1 | async-start | bytes 3981312 | tf_op jit(solution)/shard_map/all_to_all | solution.py:185
  184.5 3.2 reshape.214
  188.3 1.3 broadcast_multiply_fusion.1
  189.6 38.6 %all-to-all-done.1 = f32[4,3,162,2,128]{4,3,1,2,0:T(2,128)} async-done(((f32[4,3,162,2,128]{4,3,1,2,0:T(2,128)}), f32[4,3,162,2,128]{4,3,1,2,0:T(2,128)}, u32[]{:S(2)}, u32[]{:S(2)}) %all-to-all-start.1) | async-done | bytes 1990688 | tf_op jit(solution)/shard_map/all_to_all | solution.py:185
  228.2 3.9 %multiply_bitcast_fusion = f32[3,4,162,2,128]{4,3,0,2,1:T(2,128)} fusion(f32[4,3,162,2,128]{4,3,1,2,0:T(2,128)} %all-to-all-done.1), kind=kLoop, calls=%fused_computation.97 | loop fusion | flops 497664 | bytes 3981312 | tf_op jit(solution)/shard_map/mul | solution.py:188
  232.0 4.7 %mul.651 = f32[3,8,9,9,256]{4,0,3,2,1:T(4,128)} reshape(f32[3,4,162,2,128]{4,3,0,2,1:T(2,128)} %multiply_bitcast_fusion) | data formatting | bytes 3981312 | tf_op jit(solution)/shard_map/mul | solution.py:188
  236.7 3.3 fusion.36
  240.3 2.6 collective-permute-start.1
  243.2 3.9 %collective-permute-done = f32[3,8,1,9,256]{4,2,0,1,3:T(1,128)S(1)} collective-permute-done((f32[3,8,1,9,256]{4,2,0,1,3:T(1,128)S(1)}, f32[3,8,1,9,256]{4,2,0,1,3:T(1,128)S(1)}, u32[]{:S(2)}, u32[]{:S(2)}) %collective-permute-start) | collective-permute-done | bytes 221216 | tf_op jit(solution)/shard_map/ppermute | solution.py:45
  249.8 4.9 %fusion.46 = f32[3,8,9,256,9]{3,4,2,1,0:T(8,128)S(1)} fusion(f32[9,9,1,1,1]{1,0,4,3,2:T(8,128)S(1)} %copy-done.13, f32[3,8,9,9,256]{4,2,3,1,0:T(8,128)S(1)} %copy_multiply_fusion.4), kind=kOutput, calls=%fused_computation.66 | convolution fusion | flops 53747712 | bytes 3981636 | tf_op jit(solution)/shard_map/ij,peajl->peail/dot_general | solution.py:106
  254.8 4.2 %fusion.33 = f32[3,8,9,256,9]{3,4,2,1,0:T(8,128)S(1)} fusion(f32[9,9,1,1,1]{1,0,4,3,2:T(8,128)S(1)} %copy-done.13, f32[3,8,9,256,9]{3,4,2,1,0:T(8,128)S(1)} %fusion.46, f32[8]{0:T(128)S(1)} %copy-done.31, f32[9,9]{1,0:T(8,128)S(1)} %copy-done.17), kind=kOutput, calls=%fused_computation.49 | convolution fusion | flops 54743040 | bytes 3981992 | tf_op jit(solution)/shard_map/ji,peajl->peail/dot_general | solution.py:109
  259.0 3.9 %fusion.35 = f32[3,8,9,9,256]{4,2,3,1,0:T(8,128)S(1)} fusion(f32[9,9,1,1,1]{1,0,4,3,2:T(8,128)S(1)} %copy-done.13, f32[8]{0:T(128)S(1)} %copy-done.33, f32[9,9]{0,1:T(8,128)S(1)} %broadcast_multiply_fusion.5, f32[3,8,9,9,256]{4,2,0,1,3:T(8,128)S(1)} %fusion.25), kind=kOutput, calls=%fused_computation.52 | convolution fusion | flops 55240704 | bytes 3981992 | tf_op jit(solution)/shard_map/ij,pejbl->peibl/dot_general | solution.py:105
  262.9 5.9 %fusion.32 = f32[3,8,9,9,256]{4,2,0,1,3:T(8,128)S(1)} fusion(f32[3,8,9,256,9]{3,4,2,1,0:T(8,128)S(1)} %fusion.33, f32[8,9,9]{1,0,2:T(8,128)S(1)} %copy-done.22, f32[256]{0:T(256)S(1)} %pad_maximum_fusion.7, f32[3,8,9,1,256]{4,2,0,1,3:T(8,128)S(1)} %maximum_add_fusion.1, f32[3,8,1,9,256]{4,2,0,1,3:T(1,128)S(1)} %get-tuple-element.32, ...), kind=kOutput, calls=%fused_computation.48 | convolution fusion | flops 61212672 | bytes 8408932 | tf_op jit(solution)/shard_map/ji,pejbl->peibl/dot_general | solution.py:109
  269.1 1.8 collective-permute-start.2
  270.9 1.1 collective-permute-start.3
  272.3 4.4 %collective-permute-done.2 = f32[3,8,1,9,256]{4,2,0,1,3:T(1,128)S(1)} collective-permute-done((f32[3,8,1,9,256]{4,2,0,1,3:T(1,128)S(1)}, f32[3,8,1,9,256]{4,2,0,1,3:T(1,128)S(1)}, u32[]{:S(2)}, u32[]{:S(2)}) %collective-permute-start.2) | collective-permute-done | bytes 221216 | tf_op jit(solution)/shard_map/ppermute | solution.py:45
  279.4 1.9 multiply_reduce_fusion.1
  281.3 14.7 %all-reduce.1 = (f32[3,256]{1,0:T(4,128)}, f32[3,256]{1,0:T(4,128)}) all-reduce(f32[3,256]{1,0:T(4,128)} %get-tuple-element.8, f32[3,256]{1,0:T(4,128)} %get-tuple-element.7), channel_id=1, replica_groups=mesh['elem'=8,'mode'=4] {'elem'}, use_global_device_ids=true, to_apply=%region_4.5 | all-reduce | flops 1536 | bytes 12288 | tf_op jit(solution)/shard_map/psum | solution.py:123
  296.0 1.3 broadcast_multiply_fusion.7
  297.3 5.0 %multiply_subtract_fusion = (f32[3,8,9,9,256]{4,2,3,1,0:T(8,128)S(1)}, f32[3,8,9,9,256]{4,2,3,1,0:T(8,128)}) fusion(f32[3,256]{1,0:T(4,128)S(1)} %get-tuple-element.14, f32[3,8,9,9,256]{4,2,0,1,3:T(8,128)S(1)} %fusion.25, f32[3,8,9,1,256]{4,2,3,1,0:T(8,128)} %copy-done.7, f32[3,7,9,256]{3,2,0,1:T(8,128)} %copy-done.12, f32[3,1,9,256]{3,2,0,1:T(8,128)} %copy-done.14, ...), kind=kLoop, calls=%fused_computation.72 | loop fusion | flops 2543616 | bytes 7965696 | tf_op jit(solution)/shard_map/sub | solution.py:211
  302.3 4.9 %fusion.43 = f32[3,8,9,256,9]{3,4,2,1,0:T(8,128)S(1)} fusion(f32[9,9,1,1,1]{1,0,4,3,2:T(8,128)S(1)} %copy-done.13, f32[3,8,9,9,256]{4,2,3,1,0:T(8,128)S(1)} %get-tuple-element.25), kind=kOutput, calls=%fused_computation.62 | convolution fusion | flops 53747712 | bytes 3981636 | tf_op jit(solution)/shard_map/ij,peajl->peail/dot_general | solution.py:106
  307.2 3.4 fusion.30
  310.6 4.1 %fusion.28 = f32[3,8,9,256,9]{3,4,2,1,0:T(8,128)S(1)} fusion(f32[9,9,1,1,1]{1,0,4,3,2:T(8,128)S(1)} %copy-done.13, f32[3,8,9,256,9]{3,4,2,1,0:T(8,128)S(1)} %fusion.43, f32[8]{0:T(128)S(1)} %copy-done.32, f32[9,9]{1,0:T(8,128)S(1)} %copy-done.18), kind=kOutput, calls=%fused_computation.42 | convolution fusion | flops 54743040 | bytes 3981992 | tf_op jit(solution)/shard_map/ji,peajl->peail/dot_general | solution.py:109
  314.8 5.2 %fusion.27 = f32[3,8,9,9,256]{4,2,0,1,3:T(8,128)S(1)} fusion(f32[3,8,9,256,9]{3,4,2,1,0:T(8,128)S(1)} %fusion.28, f32[3,8,9,9,256]{4,2,3,1,0:T(8,128)S(1)} %get-tuple-element.25, f32[9,9,1,1,1]{1,0,2,3,4:T(8,128)S(1)} %copy-done.29, f32[3,8,9,9,256]{4,2,3,1,0:T(8,128)S(1)} %fusion.30, f32[256]{0:T(256)S(1)} %copy-done.40, f32[8,9,9]{1,0,2:T(8,128)S(1)} %copy-done.15), kind=kOutput, calls=%fused_computation.41 | convolution fusion | flops 56236032 | bytes 7966564 | tf_op jit(solution)/shard_map/ji,pejbl->peibl/dot_general | solution.py:109
  320.1 1.9 copy-done.6
  323.0 2.6 collective-permute-start.5
  325.6 3.0 copy.93
  328.6 4.8 %concatenate.89 = f32[3,648,2,128]{3,2,0,1:T(2,128)} reshape(f32[3,8,9,9,256]{4,0,3,2,1:T(4,128)} %copy.93) | data formatting | bytes 3981312 | tf_op jit(solution)/shard_map/concatenate | solution.py:94
  333.4 1.7 slice.176
  335.1 5.0 %copy.112 = f32[3,8,9,9,256]{4,0,3,2,1:T(4,128)} copy(f32[3,8,9,9,256]{4,2,3,1,0:T(8,128)} %get-tuple-element.26) | data formatting | bytes 3981312 | tf_op jit(solution)/shard_map/concatenate | solution.py:94
  340.1 4.5 %concatenate.105 = f32[3,648,2,128]{3,2,0,1:T(2,128)} reshape(f32[3,8,9,9,256]{4,0,3,2,1:T(4,128)} %copy.112) | data formatting | bytes 3981312 | tf_op jit(solution)/shard_map/concatenate | solution.py:94
  344.6 2.5 slice_add_fusion.1
  347.5 1.6 copy-done.1
  349.2 1.3 fusion.42
  350.5 12.0 %all-reduce = (f32[3,256]{1,0:T(4,128)S(1)}, f32[3,256]{1,0:T(4,128)S(1)}) all-reduce(f32[3,256]{1,0:T(4,128)S(1)} %get-tuple-element.6, f32[3,256]{1,0:T(4,128)S(1)} %get-tuple-element.5), channel_id=1, replica_groups=mesh['elem'=8,'mode'=4] {'elem'}, use_global_device_ids=true, to_apply=%region_8.9 | all-reduce | flops 1536 | bytes 12288 | tf_op jit(solution)/shard_map/psum | solution.py:123
  362.6 3.6 multiply_add_fusion
  366.2 2.0 copy.113
  (142 shorter events, 12.8 us)
Async XLA Ops:
  0.0 10.6 %copy-start.37 = (f32[9]{0:T(128)S(1)}, f32[9]{0:T(128)}, u32[]{:S(2)}) copy-start(f32[9]{0:T(128)} %constant.72.clone) | copy-start | bytes 112
  0.0 10.7 %copy-start.38 = (f32[8]{0:T(128)S(1)}, f32[8]{0:T(128)}, u32[]{:S(2)}) copy-start(f32[8]{0:T(128)} %param.8) | copy-start | bytes 100
  0.0 10.7 %copy-start.35 = (s32[8]{0:T(128)S(1)}, s32[8]{0:T(128)}, u32[]{:S(2)}) copy-start(s32[8]{0:T(128)} %param.9) | copy-start | bytes 100
  3.6 52.3 %all-to-all-start = ((f32[3,648,2,128]{3,2,0,1:T(2,128)}), f32[3,648,2,128]{3,2,0,1:T(2,128)S(1)}, u32[]{:S(2)}, u32[]{:S(2)}) async-start(f32[3,648,2,128]{3,2,0,1:T(2,128)} %copy.78), calls=%async_computation | async-start | bytes 3981312 | tf_op jit(solution)/shard_map/all_to_all | solution.py:152
  10.7 30.8 %copy-start.16 = (f32[9,9]{1,0:T(8,128)}, f32[9,9]{1,0:T(8,128)S(1)}, u32[]{:S(2)}) copy-start(f32[9,9]{1,0:T(8,128)S(1)} %copy.77) | copy-start | bytes 976
  13.4 65.6 %copy-start.21 = (f32[1536]{0:T(1024)}, f32[1536]{0:T(1024)S(1)}, u32[]{:S(2)}) copy-start(f32[1536]{0:T(1024)S(1)} %fusion.76) | copy-start | bytes 18436
  57.6 3.6 copy-start.11
  89.4 3.5 copy-start.10
  106.3 19.2 %copy-start.13 = (f32[9,9,1,1,1]{1,0,4,3,2:T(8,128)S(1)}, f32[9,9,1,1,1]{1,0,4,3,2:T(8,128)}, u32[]{:S(2)}) copy-start(f32[9,9,1,1,1]{1,0,4,3,2:T(8,128)} %constant.74) | copy-start | bytes 976
  125.5 11.5 %copy-start.2 = (f32[3,162,1536]{2,0,1:T(4,128)S(1)}, f32[3,162,1536]{2,0,1:T(4,128)}, u32[]{:S(2)}) copy-start(f32[3,162,1536]{2,0,1:T(4,128)} %copy.81) | copy-start | bytes 8957956
  125.5 11.5 %copy-start.3 = (f32[2,9,9,1536]{3,1,2,0:T(8,128)S(1)}, f32[2,9,9,1536]{3,1,2,0:T(8,128)}, u32[]{:S(2)}) copy-start(f32[2,9,9,1536]{3,1,2,0:T(8,128)} %copy.86) | copy-start | bytes 2985988
  125.5 11.5 %copy-start.5 = (f32[3,162,1536]{2,0,1:T(4,128)S(1)}, f32[3,162,1536]{2,0,1:T(4,128)}, u32[]{:S(2)}) copy-start(f32[3,162,1536]{2,0,1:T(4,128)} %copy.87) | copy-start | bytes 8957956
  125.5 11.5 %copy-start.30 = (f32[2]{0:T(128)S(1)}, f32[2]{0:T(128)}, u32[]{:S(2)}) copy-start(f32[2]{0:T(128)} %get-tuple-element.66) | copy-start | bytes 28
  151.3 1.9 copy-start.9
  151.7 2.5 copy-start.8
  180.1 48.1 %all-to-all-start.1 = ((f32[4,3,162,2,128]{4,3,1,2,0:T(2,128)}), f32[4,3,162,2,128]{4,3,1,2,0:T(2,128)}, u32[]{:S(2)}, u32[]{:S(2)}) async-start(f32[4,3,162,2,128]{4,3,1,2,0:T(2,128)} %pad_maximum_fusion.3), calls=%async_computation.1 | async-start | bytes 3981312 | tf_op jit(solution)/shard_map/all_to_all | solution.py:185
  240.3 6.8 %collective-permute-start = (f32[3,8,1,9,256]{4,2,0,1,3:T(1,128)S(1)}, f32[3,8,1,9,256]{4,2,0,1,3:T(1,128)S(1)}, u32[]{:S(2)}, u32[]{:S(2)}) collective-permute-start(f32[3,8,1,9,256]{4,2,0,1,3:T(1,128)S(1)} %get-tuple-element.33), channel_id=1, source_target_pairs={{0,4},{4,8},{8,12},{12,16},{16,20},{20,24},{24,28},{28,0},{1,5},{5... | collective-permute-start | bytes 663560 | tf_op jit(solution)/shard_map/ppermute | solution.py:45
  240.3 6.8 %collective-permute-start.1 = (f32[3,8,1,9,256]{4,2,0,1,3:T(1,128)S(1)}, f32[3,8,1,9,256]{4,2,0,1,3:T(1,128)S(1)}, u32[]{:S(2)}, u32[]{:S(2)}) collective-permute-start(f32[3,8,1,9,256]{4,2,0,1,3:T(1,128)S(1)} %get-tuple-element.34), channel_id=1, source_target_pairs={{4,0},{8,4},{12,8},{16,12},{20,16},{24,20},{28,24},{0,28},{5,1},{9... | collective-permute-start | bytes 663560 | tf_op jit(solution)/shard_map/ppermute | solution.py:46
  243.0 19.9 %copy-start.39 = (f32[256]{0:T(256)}, f32[256]{0:T(256)S(1)}, u32[]{:S(2)}) copy-start(f32[256]{0:T(256)S(1)} %pad_maximum_fusion.7) | copy-start | bytes 3076
  249.8 4.9 %copy-start.17 = (f32[9,9]{1,0:T(8,128)S(1)}, f32[9,9]{1,0:T(8,128)}, u32[]{:S(2)}) copy-start(f32[9,9]{1,0:T(8,128)} %copy-done.16) | copy-start | bytes 976
  249.8 4.9 %copy-start.31 = (f32[8]{0:T(128)S(1)}, f32[8]{0:T(128)}, u32[]{:S(2)}) copy-start(f32[8]{0:T(128)} %get-tuple-element.61) | copy-start | bytes 100
  254.7 4.2 %copy-start.33 = (f32[8]{0:T(128)S(1)}, f32[8]{0:T(128)}, u32[]{:S(2)}) copy-start(f32[8]{0:T(128)} %get-tuple-element.64) | copy-start | bytes 100
  258.9 4.0 %copy-start.22 = (f32[8,9,9]{1,0,2:T(8,128)S(1)}, f32[8,9,9]{1,0,2:T(8,128)}, u32[]{:S(2)}) copy-start(f32[8,9,9]{1,0,2:T(8,128)} %get-tuple-element.55) | copy-start | bytes 7780
  258.9 4.0 %copy-start.28 = (f32[9,9,1,1,1]{1,0,2,3,4:T(8,128)S(1)}, f32[9,9,1,1,1]{1,0,2,3,4:T(8,128)}, u32[]{:S(2)}) copy-start(f32[9,9,1,1,1]{1,0,2,3,4:T(8,128)} %constant.75) | copy-start | bytes 976
  262.9 9.1 %copy-start.36 = (f32[9]{0:T(128)S(1)}, f32[9]{0:T(128)}, u32[]{:S(2)}) copy-start(f32[9]{0:T(128)} %or_select_fusion) | copy-start | bytes 112
  269.1 7.6 %collective-permute-start.2 = (f32[3,8,1,9,256]{4,2,0,1,3:T(1,128)S(1)}, f32[3,8,1,9,256]{4,2,0,1,3:T(1,128)S(1)}, u32[]{:S(2)}, u32[]{:S(2)}) collective-permute-start(f32[3,8,1,9,256]{4,2,0,1,3:T(1,128)S(1)} %get-tuple-element.29), channel_id=1, source_target_pairs={{0,4},{4,8},{8,12},{12,16},{16,20},{20,24},{24,28},{28,0},{1,5},{5... | collective-permute-start | bytes 663560 | tf_op jit(solution)/shard_map/ppermute | solution.py:45
  270.9 5.8 %collective-permute-start.3 = (f32[3,8,1,9,256]{4,2,0,1,3:T(1,128)S(1)}, f32[3,8,1,9,256]{4,2,0,1,3:T(1,128)S(1)}, u32[]{:S(2)}, u32[]{:S(2)}) collective-permute-start(f32[3,8,1,9,256]{4,2,0,1,3:T(1,128)S(1)} %get-tuple-element.30), channel_id=1, source_target_pairs={{4,0},{8,4},{12,8},{16,12},{20,16},{24,20},{28,24},{0,28},{5,1},{9... | collective-permute-start | bytes 663560 | tf_op jit(solution)/shard_map/ppermute | solution.py:46
  272.1 6.2 %copy-start.19 = (f32[9,9]{0,1:T(8,128)}, f32[9,9]{0,1:T(8,128)S(1)}, u32[]{:S(2)}) copy-start(f32[9,9]{0,1:T(8,128)S(1)} %multiply_divide_fusion) | copy-start | bytes 976
  277.9 1.5 copy-start.4
  278.2 3.1 copy-start.12
  278.2 3.0 copy-start.14
  279.4 1.9 copy-start.7
  297.3 5.0 %copy-start.23 = (f32[3,256]{1,0:T(4,128)}, f32[3,256]{1,0:T(4,128)S(1)}, u32[]{:S(2)}) copy-start(f32[3,256]{1,0:T(4,128)S(1)} %get-tuple-element.14) | copy-start | bytes 9220
  302.3 12.5 %copy-start = (f32[3,8,9,9,256]{4,2,3,1,0:T(8,128)}, f32[3,8,9,9,256]{4,2,3,1,0:T(8,128)S(1)}, u32[]{:S(2)}) copy-start(f32[3,8,9,9,256]{4,2,3,1,0:T(8,128)S(1)} %get-tuple-element.25) | copy-start | bytes 5971972
  302.3 4.9 %copy-start.34 = (f32[8]{0:T(128)S(1)}, f32[8]{0:T(128)}, u32[]{:S(2)}) copy-start(f32[8]{0:T(128)} %get-tuple-element.64) | copy-start | bytes 100
  307.2 3.4 copy-start.18
  307.2 3.4 copy-start.32
  310.6 4.2 %copy-start.15 = (f32[8,9,9]{1,0,2:T(8,128)S(1)}, f32[8,9,9]{1,0,2:T(8,128)}, u32[]{:S(2)}) copy-start(f32[8,9,9]{1,0,2:T(8,128)} %get-tuple-element.56) | copy-start | bytes 7780
  310.6 4.2 %copy-start.29 = (f32[9,9,1,1,1]{1,0,2,3,4:T(8,128)S(1)}, f32[9,9,1,1,1]{1,0,2,3,4:T(8,128)}, u32[]{:S(2)}) copy-start(f32[9,9,1,1,1]{1,0,2,3,4:T(8,128)} %constant.75) | copy-start | bytes 976
  310.6 4.2 %copy-start.40 = (f32[256]{0:T(256)S(1)}, f32[256]{0:T(256)}, u32[]{:S(2)}) copy-start(f32[256]{0:T(256)} %copy-done.39) | copy-start | bytes 3076
  320.1 1.9 copy-start.6
  323.0 21.6 %collective-permute-start.4 = (f32[3,8,1,9,256]{4,2,0,1,3:T(1,128)}, f32[3,8,1,9,256]{4,2,0,1,3:T(1,128)}, u32[]{:S(2)}, u32[]{:S(2)}) collective-permute-start(f32[3,8,1,9,256]{4,2,0,1,3:T(1,128)} %get-tuple-element.23), channel_id=1, source_target_pairs={{0,4},{4,8},{8,12},{12,16},{16,20},{20,24},{24,28},{28,0},{1,5},{5... | collective-permute-start | bytes 663560 | tf_op jit(solution)/shard_map/ppermute | solution.py:45
  323.0 21.6 %collective-permute-start.5 = (f32[3,8,1,9,256]{4,2,0,1,3:T(1,128)}, f32[3,8,1,9,256]{4,2,0,1,3:T(1,128)}, u32[]{:S(2)}, u32[]{:S(2)}) collective-permute-start(f32[3,8,1,9,256]{4,2,0,1,3:T(1,128)} %get-tuple-element.24), channel_id=1, source_target_pairs={{4,0},{8,4},{12,8},{16,12},{20,16},{24,20},{28,24},{0,28},{5,1},{9... | collective-permute-start | bytes 663560 | tf_op jit(solution)/shard_map/ppermute | solution.py:46
  328.6 6.5 %copy-start.24 = (f32[3,256]{1,0:T(4,128)S(1)}, f32[3,256]{1,0:T(4,128)}, u32[]{:S(2)}) copy-start(f32[3,256]{1,0:T(4,128)} %copy-done.23) | copy-start | bytes 9220
  340.1 4.5 %copy-start.25 = (f32[3,256]{1,0:T(4,128)S(1)}, f32[3,256]{1,0:T(4,128)}, u32[]{:S(2)}) copy-start(f32[3,256]{1,0:T(4,128)} %get-tuple-element.13) | copy-start | bytes 9220
  347.1 2.0 copy-start.1
  347.2 2.0 copy-start.20
  349.1 13.4 %copy-start.26 = (f32[3,256]{1,0:T(4,128)S(1)}, f32[3,256]{1,0:T(4,128)}, u32[]{:S(2)}) copy-start(f32[3,256]{1,0:T(4,128)} %get-tuple-element.11) | copy-start | bytes 9220
  349.2 13.4 %copy-start.27 = (f32[3,256]{1,0:T(4,128)S(1)}, f32[3,256]{1,0:T(4,128)}, u32[]{:S(2)}) copy-start(f32[3,256]{1,0:T(4,128)} %get-tuple-element.12) | copy-start | bytes 9220
